TPU v7x, 512 devices: a whole 4x8x8 slice. The times are simulated.
512 devices in a mesh: node: 32 (over z_lo, x, core), group: 16 (over y, z_hi).
Axes of the slice: x: 4, y: 8, z: 8 (z_hi: 2, z_lo: 4; z = z_hi * 4 + z_lo), core: 2. Of those that a mesh axis runs over, the one named last changes fastest.
Arguments:
- tokens: bfloat16 [131072, 1024], P(('node', 'group')), may hold values from -6 to 6
- grad_out: bfloat16 [131072, 1024], P(('node', 'group')), may hold values from -1.5 to 1.5
- router_gate: float32 [131072, 4], P(('node', 'group')), may hold values from 0.1 to 1
- counts: int32 [512], P(('node', 'group')), may hold values from 1 to 2
- routes: int32 [512, 2, 4], P(('node', 'group')), may hold values from 0 to 15, as said below
- partner: int32 [32], replicated, may hold values from 0 to 31, as said below
- w_gate: bfloat16 [512, 1024, 256], P(('node', 'group')), may hold values from -0.1875 to 0.1875
- w_up: bfloat16 [512, 1024, 256], P(('node', 'group')), may hold values from -0.1875 to 0.1875
- w_down: bfloat16 [512, 256, 1024], P(('node', 'group')), may hold values from -0.375 to 0.375
Outputs:
- grad_tokens: bfloat16 [131072, 1024], P(('node', 'group'))
- grad_gate: bfloat16 [512, 1024, 256], P(('node', 'group'))
- grad_up: bfloat16 [512, 1024, 256], P(('node', 'group'))
- grad_down: bfloat16 [512, 256, 1024], P(('node', 'group'))
Inputs may be any that keep to these rules, and one draw needn't show every extreme that they name: `routes`: the 8 entries of one device name different devices of its group; every device of a group is named; in every node group one device is named by exactly 12 entries and none by more. partner pairs the nodes: partner[partner[n]] = n and partner[n] != n.
All inputs are finite; a program needn't handle non-finite values.
Results may differ from a plain program's by a relative error of at most 0.015.
Values may be sent and summed in bfloat16 or wider, within the bound.
A program may use at most 128 MiB of HBM per device.

v0:
```python
import math
import jax
import jax.numpy as jnp
from jax import lax
from jax.sharding import PartitionSpec as P


def side_by_side(arrays, axis, split_dim, concat_dim, along):
    widths = [math.prod(a.shape[along:]) for a in arrays]
    both = jnp.concatenate(
        [a.reshape(*a.shape[:along], w) for a, w in zip(arrays, widths)], axis=along
    )
    result = lax.all_to_all(both, axis, split_axis=split_dim, concat_axis=concat_dim, tiled=True)
    tiles = jnp.split(result, [sum(widths[:k]) for k in range(1, len(widths))], axis=along)
    return tuple(
        (b.reshape(*result.shape[:along], *a.shape[along:]) for a, b in zip(arrays, tiles))
    )


def sent_to_all(x, axis):
    copies = jnp.broadcast_to(x, (lax.axis_size(axis), *x.shape))
    return lax.all_to_all(copies, axis, split_axis=0, concat_axis=0, tiled=True)


def in_order(tiles, dim):
    tiles = jnp.moveaxis(tiles, 0, dim)
    dims = tiles.shape
    return tiles.reshape(*dims[:dim], dims[dim] * dims[dim + 1], *dims[dim + 2 :])


def gathered_copies(x, axis, dim):
    tiles = sent_to_all(x, axis)
    return in_order(tiles, dim)


def against(left, right):
    return lax.dot_general(
        left, right, (((1,), (1,)), ((), ())), preferred_element_type=jnp.float32
    )


def across(left, right):
    return lax.dot_general(
        left, right, (((0,), (0,)), ((), ())), preferred_element_type=jnp.float32
    )


def forward_pass(rows, w_gate, w_up):
    gate_pre = jnp.dot(rows, w_gate, preferred_element_type=jnp.float32)
    up_pre = jnp.dot(rows, w_up, preferred_element_type=jnp.float32)
    sigmoid = jax.nn.sigmoid(gate_pre)
    swish = gate_pre * sigmoid
    hidden = (swish * up_pre).astype(jnp.bfloat16)
    return (gate_pre, up_pre, sigmoid, swish, hidden)


def relocate(w_gate, w_up, w_down, partner):
    nodes = lax.axis_size("node")
    depth, width = (w_gate.shape[1], w_gate.shape[2])
    gate_parts = w_gate.reshape(nodes, depth // nodes, width)
    up_parts = w_up.reshape(nodes, depth // nodes, width)
    down_parts = w_down.reshape(nodes, width // nodes, depth)
    mixed = (
        lax.all_to_all(gate_parts, "node", split_axis=0, concat_axis=0, tiled=True),
        lax.all_to_all(up_parts, "node", split_axis=0, concat_axis=0, tiled=True),
        lax.all_to_all(down_parts, "node", split_axis=0, concat_axis=0, tiled=True),
    )
    gate_pick = jnp.take(mixed[0], partner, axis=0)
    up_pick = jnp.take(mixed[1], partner, axis=0)
    down_pick = jnp.take(mixed[2], partner, axis=0)
    placed = side_by_side((gate_pick, up_pick, down_pick), "node", 0, 0, 1)
    return (
        placed[0].reshape(depth, width),
        placed[1].reshape(depth, width),
        placed[2].reshape(width, depth),
    )


def on_device(tokens, grad_out, router_gate, counts, routes, partner, w_gate, w_up, w_down):
    group = lax.axis_size("group")
    slots_dev, topk = (routes.shape[1], routes.shape[2])
    spread = slots_dev * topk
    capacity = spread + spread // 2
    block = tokens.shape[0] // slots_dev
    depth = tokens.shape[1]
    shard_rows = slots_dev * block
    placed_gate, placed_up, placed_down = relocate(w_gate, w_up, w_down, partner)
    live_rows = (jnp.arange(shard_rows, dtype=jnp.int32) // block < counts[0])[:, None]
    masked_tok = jnp.where(live_rows, tokens, jnp.zeros((), jnp.bfloat16))
    masked_out = jnp.where(live_rows, grad_out, jnp.zeros((), jnp.bfloat16))
    table = gathered_copies(routes, "group", 0)
    myself = lax.axis_index("group")
    flat = table.reshape(group * spread)
    chosen = flat == myself
    index = jnp.argsort(jnp.where(chosen, 0, 1).astype(jnp.int32), stable=True)[:capacity]
    valid = chosen[index]
    sources = index // spread
    own_block = index % spread // topk
    column = index % topk
    targets = jnp.arange(group, dtype=jnp.int32)
    onehot = (routes[0][None, :, :] == targets[:, None, None]).astype(jnp.bfloat16)
    pick = ((sources[:, None] == targets[None, :]) & valid[:, None]).astype(jnp.bfloat16)
    wanted = sources * shard_rows + own_block * block
    column_hot = (jnp.arange(topk, dtype=jnp.int32)[None, :] == column[:, None]).astype(jnp.float32)
    empty = jnp.zeros((capacity, block, depth), jnp.bfloat16)
    tok_piece = lax.all_gather(masked_tok, "group", axis=0, tiled=True)
    out_piece = lax.all_gather(masked_out, "group", axis=0, tiled=True)
    gate_piece = lax.all_gather(
        router_gate.astype(jnp.bfloat16), "group", axis=0, tiled=True
    ).astype(jnp.float32)
    length = tok_piece.shape[0]
    inside = valid & (wanted >= 0) & (wanted + block <= length)
    offset = jnp.clip(wanted, 0, length - block)

    def take_one(where_at):
        return (
            lax.dynamic_slice_in_dim(tok_piece, where_at, block, 0),
            lax.dynamic_slice_in_dim(out_piece, where_at, block, 0),
            lax.dynamic_slice_in_dim(gate_piece, where_at, block, 0),
        )

    tok_sel, out_sel, gate_sel = jax.vmap(take_one)(offset)
    weight = jnp.sum(gate_sel * column_hot[:, None, :], axis=2)
    scaled_sel = (weight[:, :, None] * out_sel.astype(jnp.float32)).astype(jnp.bfloat16)
    keep = inside[:, None, None]
    got_tok = jnp.where(keep, tok_sel, empty)
    got_grad = jnp.where(keep, scaled_sel, empty)
    rows = got_tok.reshape(capacity * block, depth)
    grads = got_grad.reshape(capacity * block, depth)
    gate_pre, up_pre, sigmoid, swish, hidden = forward_pass(rows, placed_gate, placed_up)
    grad_hidden = against(grads, placed_down)
    grad_upre = (grad_hidden * swish).astype(jnp.bfloat16)
    grad_gpre = (grad_hidden * up_pre * sigmoid * (1.0 + gate_pre * (1.0 - sigmoid))).astype(
        jnp.bfloat16
    )
    grad_wg = across(rows, grad_gpre).astype(jnp.bfloat16)
    grad_wu = across(rows, grad_upre).astype(jnp.bfloat16)
    grad_wd = across(hidden, grads).astype(jnp.bfloat16)
    inputs_grad = (against(grad_gpre, placed_gate) + against(grad_upre, placed_up)).astype(
        jnp.bfloat16
    )
    slots = jnp.einsum(
        "rg,rsd->gsd",
        pick,
        inputs_grad.reshape(capacity, block, depth),
        preferred_element_type=jnp.float32,
    ).astype(jnp.bfloat16)
    returned = lax.all_to_all(slots, "group", split_axis=0, concat_axis=0, tiled=True)
    mine = jnp.einsum("gbk,gsd->bsd", onehot, returned, preferred_element_type=jnp.float32)
    mine = mine.astype(jnp.bfloat16).reshape(shard_rows, depth)
    grad_tokens = jnp.where(live_rows, mine, jnp.zeros((), jnp.bfloat16))
    width = placed_gate.shape[1]
    return (
        grad_tokens,
        grad_wg.reshape(1, depth, width),
        grad_wu.reshape(1, depth, width),
        grad_wd.reshape(1, width, depth),
    )


def solution(mesh):
    return jax.shard_map(
        on_device,
        mesh=mesh,
        in_specs=(
            P(("node", "group"), None),
            P(("node", "group"), None),
            P(("node", "group"), None),
            P(("node", "group")),
            P(("node", "group"), None, None),
            P(),
            P(("node", "group"), None, None),
            P(("node", "group"), None, None),
            P(("node", "group"), None, None),
        ),
        out_specs=(
            P(("node", "group"), None),
            P(("node", "group"), None, None),
            P(("node", "group"), None, None),
            P(("node", "group"), None, None),
        ),
        check_vma=False,
    )
```

profile of v0, /device:TPU:36, one launch (start us, length us, event | category | flops | bytes accessed | tf_op | source)
XLA Modules:
  0.0 643.8 jit_solution(11685429359600773166)
XLA Ops:
  8.0 2.3 broadcast_select_fusion.5
  11.1 22.8 %all_to_all.37 = s32[16,1,2,4]{3,2,1,0:T(2,128)S(1)} all-to-all(s32[16,1,2,4]{3,2,1,0:T(2,128)S(1)} %broadcast_in_dim.93), channel_id=1, replica_groups=mesh['node'=32,'group'=16] {'group'}, dimensions={0} | all-to-all | bytes 1024 | tf_op jit(solution)/shard_map/all_to_all | solution.py:22
  33.9 25.4 %all_to_all.38 = bf16[32,32,256]{2,1,0:T(8,128)(2,1)S(1)} all-to-all(bf16[32,32,256]{2,1,0:T(8,128)(2,1)S(1)} %bitcast.94), channel_id=1, replica_groups=mesh['node'=32,'group'=16] {'node'}, dimensions={0} | all-to-all | bytes 1048576 | tf_op jit(solution)/shard_map/all_to_all | solution.py:64
  59.3 6.5 %all-to-all-start.2 = ((bf16[32,32,256]{2,1,0:T(8,128)(2,1)}), bf16[32,32,256]{2,1,0:T(8,128)(2,1)S(1)}, u32[]{:S(2)}, u32[]{:S(2)}) async-start(bf16[32,32,256]{2,1,0:T(8,128)(2,1)} %bitcast.7), calls=%async_computation.2 | async-start | bytes 1048576 | tf_op jit(solution)/shard_map/all_to_all | solution.py:65
  65.8 52.1 %all_gather.9 = bf16[4096,4]{0,1:T(4,128)(2,1)S(1)} all-gather(bf16[256,4]{0,1:T(4,128)(2,1)S(1)} %convert_element_type.78), channel_id=1, replica_groups=mesh['node'=32,'group'=16] {'group'}, dimensions={0}, use_global_device_ids=true | all-gather | bytes 34816 | tf_op jit(solution)/shard_map/all_gather | solution.py:108
  118.2 11.6 %all-to-all-start.3 = ((bf16[32,8,1024]{2,1,0:T(8,128)(2,1)}), bf16[32,8,1024]{2,1,0:T(8,128)(2,1)S(1)}, u32[]{:S(2)}, u32[]{:S(2)}) async-start(bf16[32,8,1024]{2,1,0:T(8,128)(2,1)} %bitcast.8), calls=%async_computation.3 | async-start | bytes 1048576 | tf_op jit(solution)/shard_map/all_to_all | solution.py:66
  129.8 2.5 sort.17
  135.0 56.3 %all-to-all-done.3 = bf16[32,8,1024]{2,1,0:T(8,128)(2,1)S(1)} async-done(((bf16[32,8,1024]{2,1,0:T(8,128)(2,1)}), bf16[32,8,1024]{2,1,0:T(8,128)(2,1)S(1)}, u32[]{:S(2)}, u32[]{:S(2)}) %all-to-all-start.3) | async-done | bytes 524320 | tf_op jit(solution)/shard_map/all_to_all | solution.py:66
  194.8 2.1 reshape.318
  196.9 5.2 all-to-all-start.4
  202.2 15.8 %while.3 = (s32[]{:T(128)}, f32[4096,4]{0,1:T(4,128)S(1)}, s32[12,2]{0,1:T(2,128)S(1)}, f32[12,128,4]{1,2,0:T(4,128)S(1)}, s32[]{:T(128)}) while((s32[]{:T(128)}, f32[4096,4]{0,1:T(4,128)S(1)}, s32[12,2]{0,1:T(2,128)S(1)}, f32[12,128,4]{1,2,0:T(4,128)S(1)}, s32[]{:T(128)}) %tuple.54), condition=%wide.while_cond, body=%wide.while_body.sunk | while | flops 2 | bytes 4193 | solution.py:119
  218.0 21.4 %all-to-all-done.4 = bf16[32,2,12288]{2,1,0:T(2,128)(2,1)} async-done(((bf16[32,2,12288]{2,1,0:T(2,128)(2,1)}), bf16[32,2,12288]{2,1,0:T(2,128)(2,1)}, u32[]{:S(2)}, u32[]{:S(2)}) %all-to-all-start.4) | async-done | bytes 1572896 | tf_op jit(solution)/shard_map/all_to_all | solution.py:13
  239.4 8.2 %reshape.319 = bf16[32,1,24576]{2,1,0:T(2,128)(2,1)S(1)} reshape(bf16[32,2,12288]{2,1,0:T(2,128)(2,1)} %all-to-all-done.4) | data formatting | bytes 3145728
  253.0 27.4 %while.4 = (s32[]{:T(128)}, bf16[4096,1024]{1,0:T(8,128)(2,1)}, s32[12,2]{0,1:T(2,128)S(1)}, bf16[12,128,1024]{2,1,0:T(8,128)(2,1)S(1)}, s32[]{:T(128)}) while((s32[]{:T(128)}, bf16[4096,1024]{1,0:T(8,128)(2,1)}, s32[12,2]{0,1:T(2,128)S(1)}, bf16[12,128,1024]{2,1,0:T(8,128)(2,1)S(1)}, s32[]{:T(128)}) %tuple.67), condition=%wide.while_cond.1, body=%wide.while_body.1.sunk | while | flops 2 | bytes 524385 | solution.py:118
  282.1 134.0 %all-gather.5.cloned.1.call-done = bf16[4096,1024]{1,0:T(8,128)(2,1)} async-done(((bf16[256,1024]{1,0:T(8,128)(2,1)}), bf16[4096,1024]{1,0:T(8,128)(2,1)}) %all-gather.5.cloned.1.call-update) | async-done | bytes 8388624 | tf_op jit(solution)/shard_map/all_gather | solution.py:106
  416.5 27.4 %while.5 = (s32[]{:T(128)}, bf16[4096,1024]{1,0:T(8,128)(2,1)}, s32[12,2]{0,1:T(2,128)S(1)}, bf16[12,128,1024]{2,1,0:T(8,128)(2,1)S(1)}, s32[]{:T(128)}) while((s32[]{:T(128)}, bf16[4096,1024]{1,0:T(8,128)(2,1)}, s32[12,2]{0,1:T(2,128)S(1)}, bf16[12,128,1024]{2,1,0:T(8,128)(2,1)S(1)}, s32[]{:T(128)}) %tuple.68), condition=%wide.while_cond.2, body=%wide.while_body.2.sunk | while | flops 2 | bytes 524385 | solution.py:117
  443.9 3.4 fusion.5
  453.5 2.5 fusion.7
  456.1 4.3 copy.25
  460.4 7.2 %all-to-all-start.5 = ((bf16[16,128,1024]{2,1,0:T(8,128)(2,1)}), bf16[16,128,1024]{2,1,0:T(8,128)(2,1)}, u32[]{:S(2)}, u32[]{:S(2)}) async-start(bf16[16,128,1024]{2,1,0:T(8,128)(2,1)} %copy.25), calls=%async_computation.5 | async-start | bytes 8388608 | tf_op jit(solution)/shard_map/all_to_all | solution.py:148
  467.8 3.1 fusion.6
  474.6 1.9 fusion.16
  476.5 154.7 %all-to-all-done.5 = bf16[16,128,1024]{2,1,0:T(8,128)(2,1)} async-done(((bf16[16,128,1024]{2,1,0:T(8,128)(2,1)}), bf16[16,128,1024]{2,1,0:T(8,128)(2,1)}, u32[]{:S(2)}, u32[]{:S(2)}) %all-to-all-start.5) | async-done | bytes 4194336 | tf_op jit(solution)/shard_map/all_to_all | solution.py:148
  631.2 4.7 fusion.11
  (195 shorter events, 95.7 us)
Async XLA Ops:
  7.2 3.9 copy-start.10
  7.2 26.7 %copy-start.7 = (bf16[1,1024,256]{2,1,0:T(8,128)(2,1)S(1)}, bf16[1,1024,256]{2,1,0:T(8,128)(2,1)}, u32[]{:S(2)}) copy-start(bf16[1,1024,256]{2,1,0:T(8,128)(2,1)} %param.17) | copy-start | bytes 1572868
  7.2 58.6 %copy-start.9 = (f32[256,4]{0,1:T(4,128)S(1)}, f32[256,4]{0,1:T(4,128)}, u32[]{:S(2)}) copy-start(f32[256,4]{0,1:T(4,128)} %param.13) | copy-start | bytes 12292
  7.2 110.8 %copy-start.11 = (s32[32]{0:T(128)S(1)}, s32[32]{0:T(128)}, u32[]{:S(2)}) copy-start(s32[32]{0:T(128)} %param.16) | copy-start | bytes 388
  7.2 245.4 %all-gather.3.cloned.1.call-start = ((), (), s32[]{:S(2)}) async-start(), calls=%async_computation.6 | async-start | bytes 8912896 | tf_op jit(solution)/shard_map/all_gather | solution.py:107
  10.3 405.8 %all-gather.5.cloned.1.call-start = ((), (), s32[]{:S(2)}) async-start(), calls=%async_computation.7 | async-start | bytes 8912896 | tf_op jit(solution)/shard_map/all_gather | solution.py:106
  59.3 58.9 %all-to-all-start.2 = ((bf16[32,32,256]{2,1,0:T(8,128)(2,1)}), bf16[32,32,256]{2,1,0:T(8,128)(2,1)S(1)}, u32[]{:S(2)}, u32[]{:S(2)}) async-start(bf16[32,32,256]{2,1,0:T(8,128)(2,1)} %bitcast.7), calls=%async_computation.2 | async-start | bytes 1048576 | tf_op jit(solution)/shard_map/all_to_all | solution.py:65
  118.2 73.1 %all-to-all-start.3 = ((bf16[32,8,1024]{2,1,0:T(8,128)(2,1)}), bf16[32,8,1024]{2,1,0:T(8,128)(2,1)S(1)}, u32[]{:S(2)}, u32[]{:S(2)}) async-start(bf16[32,8,1024]{2,1,0:T(8,128)(2,1)} %bitcast.8), calls=%async_computation.3 | async-start | bytes 1048576 | tf_op jit(solution)/shard_map/all_to_all | solution.py:66
  196.9 42.5 %all-to-all-start.4 = ((bf16[32,2,12288]{2,1,0:T(2,128)(2,1)}), bf16[32,2,12288]{2,1,0:T(2,128)(2,1)}, u32[]{:S(2)}, u32[]{:S(2)}) async-start(bf16[32,2,12288]{2,1,0:T(2,128)(2,1)} %reshape.318), calls=%async_computation.4 | async-start | bytes 3145728 | tf_op jit(solution)/shard_map/all_to_all | solution.py:13
  280.4 1.7 copy-start
  443.9 3.4 copy-start.2
  447.3 1.0 copy-start.1
  448.4 3.0 copy-start.12
  448.4 1.4 copy-start.8
  449.4 1.9 copy-start.14
  451.3 1.0 copy-start.3
  451.3 1.1 copy-start.5
  460.4 170.8 %all-to-all-start.5 = ((bf16[16,128,1024]{2,1,0:T(8,128)(2,1)}), bf16[16,128,1024]{2,1,0:T(8,128)(2,1)}, u32[]{:S(2)}, u32[]{:S(2)}) async-start(bf16[16,128,1024]{2,1,0:T(8,128)(2,1)} %copy.25), calls=%async_computation.5 | async-start | bytes 8388608 | tf_op jit(solution)/shard_map/all_to_all | solution.py:148
  467.8 3.1 copy-start.4
  470.9 1.8 copy-start.6
  472.7 1.8 copy-start.13
  472.7 1.9 copy-start.15
Sparse Core Ops, SparseCore 0:
  11.8 210.6 all-gather.2
  226.3 189.8 all-gather.4
where the time goes:
time: 646 us; the launch traced here: 644 us
  waiting for transfers between devices  367 us (57%)
  blocking collectives  100 us (15%)
  local copies, waits for them, and re-layouts  96.8 us (15%)
  starting transfers between devices  30.6 us (5%)
  matrix products  18.4 us (3%)
  between operations  15.2 us (2%)
  other arithmetic  14.8 us (2%)
    all_to_all x1, waiting for transfers between devices, on_device(): lax.all_to_all(slots, 'group', split_axis=0, concat_axis=0, tiled=True)  155 us
    all_gather x1, waiting for transfers between devices, on_device(): tok_piece = lax.all_gather(masked_tok, 'group', axis=0, tiled=True)  134 us
    gather x108, local copies, waits for them, and re-layouts  70 us
    all_to_all x1, waiting for transfers between devices, relocate(): lax.all_to_all(down_parts, 'node', split_axis=0, concat_axis=0, tiled=True)  56.3 us
    all_gather x1, blocking collectives, on_device(): lax.all_gather(router_gate.astype(jnp.bfloat16), 'group', axis=0, tiled=T...  52.1 us
    all_to_all x1, blocking collectives, relocate(): lax.all_to_all(gate_parts, 'node', split_axis=0, concat_axis=0, tiled=True)  25.4 us
    all_to_all x1, blocking collectives, sent_to_all(): return lax.all_to_all(copies, axis, split_axis=0, concat_axis=0, tiled=True)  22.8 us
    all_to_all x1, waiting for transfers between devices, side_by_side(): lax.all_to_all(both, axis, split_axis=split_dim, concat_axis=concat_dim,...  21.4 us
  transfers between devices with their start and end apart: 6, of which 4 were waited for; matrix products, arithmetic and copies ran while one was open for 12% of the time, Pallas kernels for 0%

commit v1 on v0

--- a/solution.py
+++ b/solution.py
@@ -3,6 +3,7 @@
 import jax.numpy as jnp
 from jax import lax
 from jax.sharding import PartitionSpec as P
+from jax.lax import all_to_all, axis_size
 
 
 def side_by_side(arrays, axis, split_dim, concat_dim, along):
@@ -103,7 +104,9 @@
     wanted = sources * shard_rows + own_block * block
     column_hot = (jnp.arange(topk, dtype=jnp.int32)[None, :] == column[:, None]).astype(jnp.float32)
     empty = jnp.zeros((capacity, block, depth), jnp.bfloat16)
-    tok_piece = lax.all_gather(masked_tok, "group", axis=0, tiled=True)
+    tok_piece = jnp.concatenate(
+        all_to_all(jnp.stack(axis_size("group") * [masked_tok], axis=0), "group", 0, 0), axis=0
+    )
     out_piece = lax.all_gather(masked_out, "group", axis=0, tiled=True)
     gate_piece = lax.all_gather(
         router_gate.astype(jnp.bfloat16), "group", axis=0, tiled=True

time: 646 us -> 845 us (1.31)
  the two profiles are of different devices: /device:TPU:36 before, /device:TPU:48 now
where the time goes in v1:
time: 845 us; the launch traced here: 843 us
  blocking collectives  469 us (56%)
  waiting for transfers between devices  182 us (22%)
  local copies, waits for them, and re-layouts  101 us (12%)
  starting transfers between devices  43.1 us (5%)
  matrix products  18.4 us (2%)
  between operations  15.2 us (2%)
  other arithmetic  13.4 us (2%)
    all_gather x1, blocking collectives, on_device(): lax.all_gather(router_gate.astype(jnp.bfloat16), 'group', axis=0, tiled=T...  422 us
    all_to_all x1, waiting for transfers between devices, on_device(): lax.all_to_all(slots, 'group', split_axis=0, concat_axis=0, tiled=True)  129 us
    gather x108, local copies, waits for them, and re-layouts  69.2 us
    all_to_all x1, waiting for transfers between devices, side_by_side(): lax.all_to_all(both, axis, split_axis=split_dim, concat_axis=concat_dim,...  35.8 us
    all_to_all x1, blocking collectives, relocate(): lax.all_to_all(gate_parts, 'node', split_axis=0, concat_axis=0, tiled=True)  26.1 us
    all_to_all x1, blocking collectives, relocate(): lax.all_to_all(up_parts, 'node', split_axis=0, concat_axis=0, tiled=True)  20.5 us
  transfers between devices with their start and end apart: 6, of which 4 were waited for; matrix products, arithmetic and copies ran while one was open for 9% of the time, Pallas kernels for 0%

profile of v1, /device:TPU:48, one launch (start us, length us, event | category | flops | bytes accessed | tf_op | source)
XLA Modules:
  0.0 842.6 jit_solution(5818984912092365314)
XLA Ops:
  7.2 26.1 %all_to_all.42 = bf16[32,32,256]{2,1,0:T(8,128)(2,1)S(1)} all-to-all(bf16[32,32,256]{2,1,0:T(8,128)(2,1)} %bitcast.95), channel_id=1, replica_groups=mesh['node'=32,'group'=16] {'node'}, dimensions={0} | all-to-all | bytes 1048576 | tf_op jit(solution)/shard_map/all_to_all | solution.py:65
  33.2 20.5 %all_to_all.43 = bf16[32,32,256]{2,1,0:T(8,128)(2,1)S(1)} all-to-all(bf16[32,32,256]{2,1,0:T(8,128)(2,1)} %bitcast.96), channel_id=1, replica_groups=mesh['node'=32,'group'=16] {'node'}, dimensions={0} | all-to-all | bytes 1048576 | tf_op jit(solution)/shard_map/all_to_all | solution.py:66
  53.8 4.6 all-to-all-start.3
  60.4 13.9 %all-to-all-done.3 = bf16[32,8,1024]{2,1,0:T(8,128)(2,1)S(1)} async-done(((bf16[32,8,1024]{2,1,0:T(8,128)(2,1)}), bf16[32,8,1024]{2,1,0:T(8,128)(2,1)S(1)}, u32[]{:S(2)}, u32[]{:S(2)}) %all-to-all-start.3) | async-done | bytes 524320 | tf_op jit(solution)/shard_map/all_to_all | solution.py:67
  74.9 12.7 %all-to-all-start = ((s32[16,1,2,4]{3,2,1,0:T(2,128)}), s32[16,1,2,4]{3,2,1,0:T(2,128)S(1)}, u32[]{:S(2)}, u32[]{:S(2)}) async-start(s32[16,1,2,4]{3,2,1,0:T(2,128)} %broadcast_in_dim.93), calls=%async_computation | async-start | bytes 32768 | tf_op jit(solution)/shard_map/all_to_all | solution.py:23
  91.2 2.1 reshape.324
  93.3 3.4 all-to-all-done
  96.7 4.6 all-to-all-start.4
  102.9 35.8 %all-to-all-done.4 = bf16[32,2,12288]{2,1,0:T(2,128)(2,1)S(1)} async-done(((bf16[32,2,12288]{2,1,0:T(2,128)(2,1)}), bf16[32,2,12288]{2,1,0:T(2,128)(2,1)S(1)}, u32[]{:S(2)}, u32[]{:S(2)}) %all-to-all-start.4) | async-done | bytes 1572896 | tf_op jit(solution)/shard_map/all_to_all | solution.py:14
  138.8 4.3 stack.2
  143.1 8.9 %all-to-all-start.5 = ((bf16[16,256,1024]{2,1,0:T(8,128)(2,1)}), bf16[16,256,1024]{2,1,0:T(8,128)(2,1)}, u32[]{:S(2)}, u32[]{:S(2)}) async-start(bf16[16,256,1024]{2,1,0:T(8,128)(2,1)} %stack.2), calls=%async_computation.5 | async-start | bytes 16777216 | tf_op jit(solution)/shard_map/all_to_all | solution.py:108
  152.7 422.0 %all_gather.6 = bf16[4096,4]{0,1:T(4,128)(2,1)S(1)} all-gather(bf16[256,4]{0,1:T(4,128)(2,1)S(1)} %convert_element_type.78), channel_id=1, replica_groups=mesh['node'=32,'group'=16] {'group'}, dimensions={0}, use_global_device_ids=true | all-gather | bytes 34816 | tf_op jit(solution)/shard_map/all_gather | solution.py:111
  574.9 2.5 sort.17
  578.2 15.8 %while.3 = (s32[]{:T(128)}, f32[4096,4]{0,1:T(4,128)S(1)}, s32[12,2]{0,1:T(2,128)S(1)}, f32[12,128,4]{1,2,0:T(4,128)S(1)}, s32[]{:T(128)}) while((s32[]{:T(128)}, f32[4096,4]{0,1:T(4,128)S(1)}, s32[12,2]{0,1:T(2,128)S(1)}, f32[12,128,4]{1,2,0:T(4,128)S(1)}, s32[]{:T(128)}) %tuple.54), condition=%wide.while_cond, body=%wide.while_body.sunk | while | flops 2 | bytes 4193 | solution.py:122
  594.1 8.2 reshape.325
  607.7 26.6 %while.5 = (s32[]{:T(128)}, bf16[4096,1024]{1,0:T(8,128)(2,1)}, s32[12,2]{0,1:T(2,128)S(1)}, bf16[12,128,1024]{2,1,0:T(8,128)(2,1)S(1)}, s32[]{:T(128)}) while((s32[]{:T(128)}, bf16[4096,1024]{1,0:T(8,128)(2,1)}, s32[12,2]{0,1:T(2,128)S(1)}, bf16[12,128,1024]{2,1,0:T(8,128)(2,1)S(1)}, s32[]{:T(128)}) %tuple.65), condition=%wide.while_cond.2, body=%wide.while_body.2.sunk | while | flops 2 | bytes 524385 | solution.py:120
  636.4 27.4 %while.4 = (s32[]{:T(128)}, bf16[4096,1024]{1,0:T(8,128)(2,1)}, s32[12,2]{0,1:T(2,128)S(1)}, bf16[12,128,1024]{2,1,0:T(8,128)(2,1)S(1)}, s32[]{:T(128)}) while((s32[]{:T(128)}, bf16[4096,1024]{1,0:T(8,128)(2,1)}, s32[12,2]{0,1:T(2,128)S(1)}, bf16[12,128,1024]{2,1,0:T(8,128)(2,1)S(1)}, s32[]{:T(128)}) %tuple.66), condition=%wide.while_cond.1, body=%wide.while_body.1.sunk | while | flops 2 | bytes 524385 | solution.py:121
  663.8 3.4 fusion.5
  673.4 2.5 fusion.7
  675.9 4.3 copy.25
  680.3 12.3 %all-to-all-start.6 = ((bf16[16,128,1024]{2,1,0:T(8,128)(2,1)}), bf16[16,128,1024]{2,1,0:T(8,128)(2,1)}, u32[]{:S(2)}, u32[]{:S(2)}) async-start(bf16[16,128,1024]{2,1,0:T(8,128)(2,1)} %copy.25), calls=%async_computation.6 | async-start | bytes 8388608 | tf_op jit(solution)/shard_map/all_to_all | solution.py:151
  692.7 3.1 fusion.6
  701.4 128.6 %all-to-all-done.6 = bf16[16,128,1024]{2,1,0:T(8,128)(2,1)} async-done(((bf16[16,128,1024]{2,1,0:T(8,128)(2,1)}), bf16[16,128,1024]{2,1,0:T(8,128)(2,1)}, u32[]{:S(2)}, u32[]{:S(2)}) %all-to-all-start.6) | async-done | bytes 4194336 | tf_op jit(solution)/shard_map/all_to_all | solution.py:151
  830.0 4.7 fusion.11
  (199 shorter events, 98.3 us)
Async XLA Ops:
  7.2 51.2 %copy-start.13 = (s32[32]{0:T(128)S(1)}, s32[32]{0:T(128)}, u32[]{:S(2)}) copy-start(s32[32]{0:T(128)} %param.16) | copy-start | bytes 388
  53.8 20.5 %all-to-all-start.3 = ((bf16[32,8,1024]{2,1,0:T(8,128)(2,1)}), bf16[32,8,1024]{2,1,0:T(8,128)(2,1)S(1)}, u32[]{:S(2)}, u32[]{:S(2)}) async-start(bf16[32,8,1024]{2,1,0:T(8,128)(2,1)} %bitcast.97), calls=%async_computation.3 | async-start | bytes 1048576 | tf_op jit(solution)/shard_map/all_to_all | solution.py:67
  58.4 15.9 %copy-start.12 = (s32[1,2,4]{2,1,0:T(2,128)S(1)}, s32[1,2,4]{2,1,0:T(2,128)}, u32[]{:S(2)}) copy-start(s32[1,2,4]{2,1,0:T(2,128)} %param.15) | copy-start | bytes 100
  74.9 21.8 %all-to-all-start = ((s32[16,1,2,4]{3,2,1,0:T(2,128)}), s32[16,1,2,4]{3,2,1,0:T(2,128)S(1)}, u32[]{:S(2)}, u32[]{:S(2)}) async-start(s32[16,1,2,4]{3,2,1,0:T(2,128)} %broadcast_in_dim.93), calls=%async_computation | async-start | bytes 32768 | tf_op jit(solution)/shard_map/all_to_all | solution.py:23
  93.3 8.7 %copy-start.8 = (bf16[256,1024]{1,0:T(8,128)(2,1)S(1)}, bf16[256,1024]{1,0:T(8,128)(2,1)}, u32[]{:S(2)}) copy-start(bf16[256,1024]{1,0:T(8,128)(2,1)} %param.12) | copy-start | bytes 1572868
  93.3 8.7 %copy-start.9 = (bf16[256,1024]{1,0:T(8,128)(2,1)S(1)}, bf16[256,1024]{1,0:T(8,128)(2,1)}, u32[]{:S(2)}) copy-start(bf16[256,1024]{1,0:T(8,128)(2,1)} %param.11) | copy-start | bytes 1572868
  96.7 42.1 %all-to-all-start.4 = ((bf16[32,2,12288]{2,1,0:T(2,128)(2,1)}), bf16[32,2,12288]{2,1,0:T(2,128)(2,1)S(1)}, u32[]{:S(2)}, u32[]{:S(2)}) async-start(bf16[32,2,12288]{2,1,0:T(2,128)(2,1)} %reshape.324), calls=%async_computation.4 | async-start | bytes 3145728 | tf_op jit(solution)/shard_map/all_to_all | solution.py:14
  138.8 4.3 copy-start.1
  143.1 9.6 %copy-start.11 = (f32[256,4]{0,1:T(4,128)S(1)}, f32[256,4]{0,1:T(4,128)}, u32[]{:S(2)}) copy-start(f32[256,4]{0,1:T(4,128)} %param.13) | copy-start | bytes 12292
  143.1 464.2 %all-to-all-start.5 = ((bf16[16,256,1024]{2,1,0:T(8,128)(2,1)}), bf16[16,256,1024]{2,1,0:T(8,128)(2,1)}, u32[]{:S(2)}, u32[]{:S(2)}) async-start(bf16[16,256,1024]{2,1,0:T(8,128)(2,1)} %stack.2), calls=%async_computation.5 | async-start | bytes 16777216 | tf_op jit(solution)/shard_map/all_to_all | solution.py:108
  152.0 484.0 %all-gather.2.cloned.1.call-start = ((), (), s32[]{:S(2)}) async-start(), calls=%async_computation.7 | async-start | bytes 8912896 | tf_op jit(solution)/shard_map/all_gather | solution.py:110
  634.3 1.7 copy-start
  663.8 3.4 copy-start.3
  667.2 1.0 copy-start.2
  668.2 3.0 copy-start.14
  668.2 1.4 copy-start.10
  669.2 1.9 copy-start.16
  671.2 1.0 copy-start.4
  671.2 1.2 copy-start.6
  680.3 149.8 %all-to-all-start.6 = ((bf16[16,128,1024]{2,1,0:T(8,128)(2,1)}), bf16[16,128,1024]{2,1,0:T(8,128)(2,1)}, u32[]{:S(2)}, u32[]{:S(2)}) async-start(bf16[16,128,1024]{2,1,0:T(8,128)(2,1)} %copy.25), calls=%async_computation.6 | async-start | bytes 8388608 | tf_op jit(solution)/shard_map/all_to_all | solution.py:151
  692.7 3.1 copy-start.7
  695.8 1.8 copy-start.5
  697.6 1.8 copy-start.15
  697.6 1.9 copy-start.17
Sparse Core Ops, SparseCore 0:
  156.6 399.4 all-gather.1
